TPU v7x, 32 devices: a whole 2x2x4 slice. The times are simulated.
32 devices in a mesh: az: 4 (over x, core), rad: 8 (over z, y).
Axes of the slice: x: 2, y: 2, z: 4, core: 2. Of those that a mesh axis runs over, the one named last changes fastest.
Arguments:
- fields: float32 [4, 16, 64, 512], P(None, None, 'rad', 'az'), may hold values from -6 to 6, as said below
- shifts: int32 [16, 64], P(None, 'rad'), may hold values from 0 to 511, as said below
- courant: float32 [16, 64], P(None, 'rad'), may hold values from -0.45 to 0.45
Outputs:
- advanced: float32 [4, 16, 64, 512], P(None, None, 'rad', 'az')
Inputs may be any that keep to these rules, and one draw needn't show every extreme that they name: fields 0 and 1 (velocities) lie in the range; fields 2 and 3 (energy, density) lie between 0.5 and 2. `shifts`: any whole shift of a cycle in cells.
All inputs are finite; a program needn't handle non-finite values.
Results may differ from a plain program's by a relative error of at most 0.0003.
Values sent between devices are 32-bit elements; how exact they have to be, the bound alone decides.
A program may use at most 64 MiB of HBM per device.

v0:
```python
import math

import jax
import jax.numpy as jnp
from jax import lax
from jax.sharding import PartitionSpec as P

inner_radius = 0.4
adiabatic = 1.4


def passed_along(block, axis, distance):
    devices = range(lax.axis_size(axis))
    route = [((i - distance) % len(devices), i) for i in devices]
    return lax.ppermute(block, axis, route)


def with_halo(x, sides, width):
    for axis, dim in sides:
        size, length = (lax.axis_size(axis), x.shape[dim])
        up = [(i, (i + 1) % size) for i in range(size)]
        down = [(j, i) for i, j in up]
        last = lax.slice_in_dim(x, length - width, length, axis=dim)
        leading = lax.slice_in_dim(x, 0, width, axis=dim)
        before = lax.ppermute(last, axis, up)
        after = lax.ppermute(leading, axis, down)
        x = jnp.concatenate([before, x, after], axis=dim)
    return x


def minmod(left, right):
    return 0.5 * (jnp.sign(left) + jnp.sign(right)) * jnp.minimum(jnp.abs(left), jnp.abs(right))


def limited(extended, courant_cycle):
    differences = extended[..., 1:] - extended[..., :-1]
    slopes = minmod(differences[..., :-1], differences[..., 1:])
    centers = extended[..., 1:-1]
    flux_plus = courant_cycle * (centers[..., :-1] + 0.5 * (1.0 - courant_cycle) * slopes[..., :-1])
    flux_minus = courant_cycle * (centers[..., 1:] - 0.5 * (1.0 + courant_cycle) * slopes[..., 1:])
    face_flux = jnp.where(courant_cycle >= 0.0, flux_plus, flux_minus)
    return extended[..., 2:-2] - (face_flux[..., 1:] - face_flux[..., :-1])


def center(field):
    return field[..., 1:-1, 1:-1]


def across_az(field):
    return field[..., 1:-1, 2:] - field[..., 1:-1, :-2]


def across_rad(field):
    return field[..., 2:, 1:-1] - field[..., :-2, 1:-1]


def laplace(field, phi_width, rad_step):
    middle = center(field)
    along_az = (field[..., 1:-1, 2:] + field[..., 1:-1, :-2] - 2.0 * middle) / (
        phi_width * phi_width
    )
    along_rad = (field[..., 2:, 1:-1] + field[..., :-2, 1:-1] - 2.0 * middle) / (
        rad_step * rad_step
    )
    return along_az + along_rad


def stencil(padded, density, radius, phi_count, rad_count):
    phi_step = 2.0 * math.pi / phi_count
    rad_step = 1.0 / rad_count
    spacing = min(rad_step, inner_radius * phi_step)
    time_step = 0.2 * spacing
    viscosity = 0.05 * spacing * spacing / time_step
    radial_vel = padded[0]
    azim_vel = padded[1]
    energy = padded[2]
    pressure = (adiabatic - 1.0) * energy
    phi_width = radius * phi_step
    radial_mid = center(radial_vel)
    azim_mid = center(azim_vel)
    energy_mid = center(energy)
    radial_new = radial_mid + time_step * (
        -across_rad(pressure) * (0.5 / rad_step) / density
        + viscosity * laplace(radial_vel, phi_width, rad_step)
        + azim_mid * azim_mid / radius
        - 1.0 / (radius * radius)
    )
    azim_new = azim_mid + time_step * (
        -across_az(pressure) * 0.5 / (phi_width * density)
        + viscosity * laplace(azim_vel, phi_width, rad_step)
        - radial_mid * azim_mid / radius
    )
    divergence = (
        across_rad(radial_vel) * (0.5 / rad_step)
        + across_az(azim_vel) * 0.5 / phi_width
        + radial_mid / radius
    )
    energy_new = energy_mid - time_step * (adiabatic - 1.0) * energy_mid * divergence
    return (radial_new, azim_new, energy_new)


def barrel_roll(values, amounts, largest):
    for bit_number in range(largest.bit_length()):
        rolled = jnp.roll(values, 1 << bit_number, axis=-1)
        chosen = amounts // (1 << bit_number) % 2 == 1
        values = jnp.where(chosen[:, :, None], rolled, values)
    return values


def move_owners(placed, owner_steps, az_count):
    for bit_number in range(az_count.bit_length() - 1):
        arrived = passed_along(placed, "az", 1 << bit_number)
        chosen = owner_steps // (1 << bit_number) % 2 == 1
        placed = jnp.where(chosen[None, :, :, None], arrived, placed)
    return placed


def shards(fields, shifts, courant):
    az_cells = fields.shape[3]
    rad_cells = fields.shape[2]
    az_count = lax.axis_size("az")
    rad_count = lax.axis_size("rad")
    phi_count = az_cells * az_count
    rad_total = rad_cells * rad_count
    rad_pos = lax.axis_index("rad")
    global_rows = (rad_pos * rad_cells + jnp.arange(rad_cells, dtype=jnp.int32)).astype(jnp.float32)
    radius = (inner_radius + (global_rows + 0.5) * (1.0 / rad_total))[:, None]
    padded = with_halo(fields[0:3], (("az", 3), ("rad", 2)), 1)
    lower_rim = jnp.where(rad_pos == 0, padded[..., 1:2, :], padded[..., 0:1, :])
    upper_rim = jnp.where(rad_pos == rad_count - 1, padded[..., -2:-1, :], padded[..., -1:, :])
    padded = jnp.concatenate([lower_rim, padded[..., 1:-1, :], upper_rim], axis=2)
    radial_new, azim_new, energy_new = stencil(padded, fields[3], radius, phi_count, rad_total)
    moved = jnp.stack([radial_new, azim_new, energy_new, fields[3]])
    owner_steps = shifts // az_cells
    cell_steps = shifts % az_cells
    previous = passed_along(moved, "az", 1)
    paired = jnp.concatenate([previous, moved], axis=-1)
    paired = barrel_roll(paired, cell_steps, az_cells - 1)
    placed = paired[..., az_cells:]
    placed = move_owners(placed, owner_steps, az_count)
    extended = with_halo(placed, (("az", 3),), 2)
    result = limited(extended, courant[:, :, None])
    return result


def solution(mesh):
    return jax.shard_map(
        shards,
        mesh=mesh,
        in_specs=(P(None, None, "rad", "az"), P(None, "rad"), P(None, "rad")),
        out_specs=P(None, None, "rad", "az"),
        check_vma=False,
    )
```

profile of v0, /device:TPU:0, one launch (start us, length us, event | category | flops | bytes accessed | tf_op | source)
XLA Modules:
  0.0 54.1 jit_solution(16000206774610293595)
XLA Ops:
  0.0 1.2 %fusion.60 = (f32[3,16,8,1]{3,2,1,0:T(8,128)S(1)}, f32[3,16,8,1]{3,2,1,0:T(8,128)S(1)}) fusion(f32[4,16,8,128]{3,2,1,0:T(8,128)} %param.3), kind=kLoop, calls=%fused_computation.158 | loop fusion | bytes 6144 | tf_op jit(solution)/shard_map/slice | solution.py:23
  1.2 0.5 %collective-permute-start = (f32[3,16,8,1]{3,2,1,0:T(8,128)S(1)}, f32[3,16,8,1]{3,2,1,0:T(8,128)S(1)}, u32[]{:S(2)}, u32[]{:S(2)}) collective-permute-start(f32[3,16,8,1]{3,2,1,0:T(8,128)S(1)} %get-tuple-element.16), channel_id=1, source_target_pairs={{0,8},{8,16},{16,24},{24,0},{1,9},{9,17},{17,25},{25,1},{2,10},{10... | collective-permute-start | bytes 4616 | tf_op jit(solution)/shard_map/ppermute | solution.py:25
  1.7 2.0 %collective-permute-start.1 = (f32[3,16,8,1]{3,2,1,0:T(8,128)S(1)}, f32[3,16,8,1]{3,2,1,0:T(8,128)S(1)}, u32[]{:S(2)}, u32[]{:S(2)}) collective-permute-start(f32[3,16,8,1]{3,2,1,0:T(8,128)S(1)} %get-tuple-element.17), channel_id=1, source_target_pairs={{8,0},{16,8},{24,16},{0,24},{9,1},{17,9},{25,17},{1,25},{10,2},{18... | collective-permute-start | bytes 4616 | tf_op jit(solution)/shard_map/ppermute | solution.py:26
  3.7 3.3 %collective-permute-done = f32[3,16,8,1]{3,2,1,0:T(8,128)S(1)} collective-permute-done((f32[3,16,8,1]{3,2,1,0:T(8,128)S(1)}, f32[3,16,8,1]{3,2,1,0:T(8,128)S(1)}, u32[]{:S(2)}, u32[]{:S(2)}) %collective-permute-start) | collective-permute-done | bytes 1568 | tf_op jit(solution)/shard_map/ppermute | solution.py:25
  7.0 1.9 %collective-permute-done.1 = f32[3,16,8,1]{3,2,1,0:T(8,128)S(1)} collective-permute-done((f32[3,16,8,1]{3,2,1,0:T(8,128)S(1)}, f32[3,16,8,1]{3,2,1,0:T(8,128)S(1)}, u32[]{:S(2)}, u32[]{:S(2)}) %collective-permute-start.1) | collective-permute-done | bytes 1568 | tf_op jit(solution)/shard_map/ppermute | solution.py:26
  8.9 0.2 pad_maximum_fusion.6
  9.2 1.6 %collective-permute-start.2 = (f32[3,16,1,130]{3,2,1,0:T(1,128)S(1)}, f32[3,16,1,130]{3,2,1,0:T(1,128)S(1)}, u32[]{:S(2)}, u32[]{:S(2)}) collective-permute-start(f32[3,16,1,130]{3,2,1,0:T(1,128)S(1)} %pad_maximum_fusion.6), channel_id=1, source_target_pairs={{0,1},{1,2},{2,3},{3,4},{4,5},{5,6},{6,7},{7,0},{8,9},{9,10},{10,1... | collective-permute-start | bytes 74888 | tf_op jit(solution)/shard_map/ppermute | solution.py:25
  10.7 5.7 %collective-permute-done.2 = f32[3,16,1,130]{3,2,1,0:T(1,128)S(1)} collective-permute-done((f32[3,16,1,130]{3,2,1,0:T(1,128)S(1)}, f32[3,16,1,130]{3,2,1,0:T(1,128)S(1)}, u32[]{:S(2)}, u32[]{:S(2)}) %collective-permute-start.2) | collective-permute-done | bytes 24992 | tf_op jit(solution)/shard_map/ppermute | solution.py:25
  16.5 0.2 broadcast_select_fusion.3
  16.7 1.8 %collective-permute-start.3 = (f32[3,16,1,130]{3,2,1,0:T(1,128)S(1)}, f32[3,16,1,130]{3,2,1,0:T(1,128)S(1)}, u32[]{:S(2)}, u32[]{:S(2)}) collective-permute-start(f32[3,16,1,130]{3,2,1,0:T(1,128)S(1)} %get-tuple-element.8), channel_id=1, source_target_pairs={{1,0},{2,1},{3,2},{4,3},{5,4},{6,5},{7,6},{0,7},{9,8},{10,9},{11,1... | collective-permute-start | bytes 74888 | tf_op jit(solution)/shard_map/ppermute | solution.py:26
  18.5 2.3 %collective-permute-done.3 = f32[3,16,1,130]{3,2,1,0:T(1,128)S(1)} collective-permute-done((f32[3,16,1,130]{3,2,1,0:T(1,128)S(1)}, f32[3,16,1,130]{3,2,1,0:T(1,128)S(1)}, u32[]{:S(2)}, u32[]{:S(2)}) %collective-permute-start.3) | collective-permute-done | bytes 24992 | tf_op jit(solution)/shard_map/ppermute | solution.py:26
  20.9 0.4 pad_maximum_fusion
  21.3 0.2 add_bitcast_fusion
  21.5 0.2 fusion.14
  21.9 0.6 %copy-done.2 = s32[16,8]{0,1:T(8,128)S(1)} copy-done((s32[16,8]{0,1:T(8,128)S(1)}, s32[16,8]{0,1:T(8,128)}, u32[]{:S(2)}) %copy-start.2) | copy-done | bytes 536
  22.5 0.1 copy.12
  22.8 0.1 copy.9
  22.9 0.1 copy.8
  23.0 0.1 copy.7
  23.2 0.1 slice.253
  23.3 4.4 %collective-permute-done.4 = f32[4,16,8,128]{3,2,1,0:T(8,128)S(1)} collective-permute-done((f32[4,16,8,128]{3,2,1,0:T(8,128)S(1)}, f32[4,16,8,128]{3,2,1,0:T(8,128)S(1)}, u32[]{:S(2)}, u32[]{:S(2)}) %collective-permute-start.4) | collective-permute-done | bytes 262176 | tf_op jit(solution)/shard_map/ppermute | solution.py:15
  27.7 0.2 maximum_select_fusion
  27.9 0.1 slice.255
  28.1 0.2 maximum_select_fusion.1
  28.3 0.1 slice.257
  28.4 0.2 maximum_select_fusion.2
  28.7 0.1 slice.259
  28.8 0.2 maximum_select_fusion.3
  29.0 0.1 slice.261
  29.2 0.2 maximum_select_fusion.4
  29.4 0.1 slice.263
  29.5 0.2 maximum_select_fusion.5
  29.8 0.1 slice.265
  29.9 0.2 slice_select_fusion
  30.1 0.1 copy.5
  30.2 5.7 %collective-permute-done.5 = f32[4,16,8,128]{3,2,1,0:T(8,128)S(1)} collective-permute-done((f32[4,16,8,128]{3,2,1,0:T(8,128)S(1)}, f32[4,16,8,128]{3,2,1,0:T(8,128)S(1)}, u32[]{:S(2)}, u32[]{:S(2)}) %collective-permute-start.5) | collective-permute-done | bytes 262176 | tf_op jit(solution)/shard_map/ppermute | solution.py:15
  35.9 0.1 broadcast_select_fusion
  36.0 2.0 %collective-permute-start.6 = (f32[4,16,8,128]{3,2,1,0:T(8,128)S(1)}, f32[4,16,8,128]{3,2,1,0:T(8,128)S(1)}, u32[]{:S(2)}, u32[]{:S(2)}) collective-permute-start(f32[4,16,8,128]{3,2,1,0:T(8,128)S(1)} %broadcast_select_fusion), channel_id=1, source_target_pairs={{16,0},{24,8},{0,16},{8,24},{17,1},{25,9},{1,17},{9,25},{18,2},{26... | collective-permute-start | bytes 786440 | tf_op jit(solution)/shard_map/ppermute | solution.py:15
  38.1 5.8 %collective-permute-done.6 = f32[4,16,8,128]{3,2,1,0:T(8,128)S(1)} collective-permute-done((f32[4,16,8,128]{3,2,1,0:T(8,128)S(1)}, f32[4,16,8,128]{3,2,1,0:T(8,128)S(1)}, u32[]{:S(2)}, u32[]{:S(2)}) %collective-permute-start.6) | collective-permute-done | bytes 262176 | tf_op jit(solution)/shard_map/ppermute | solution.py:15
  43.8 0.1 broadcast_select_fusion.1
  43.9 0.1 fusion.59
  44.1 1.7 %collective-permute-start.8 = (f32[4,16,8,2]{3,2,1,0:T(8,128)S(1)}, f32[4,16,8,2]{3,2,1,0:T(8,128)S(1)}, u32[]{:S(2)}, u32[]{:S(2)}) collective-permute-start(f32[4,16,8,2]{3,2,1,0:T(8,128)S(1)} %get-tuple-element.15), channel_id=1, source_target_pairs={{8,0},{16,8},{24,16},{0,24},{9,1},{17,9},{25,17},{1,25},{10,2},{18... | collective-permute-start | bytes 12296 | tf_op jit(solution)/shard_map/ppermute | solution.py:26
  46.2 5.7 %collective-permute-done.7 = f32[4,16,8,2]{3,2,1,0:T(8,128)S(1)} collective-permute-done((f32[4,16,8,2]{3,2,1,0:T(8,128)S(1)}, f32[4,16,8,2]{3,2,1,0:T(8,128)S(1)}, u32[]{:S(2)}, u32[]{:S(2)}) %collective-permute-start.7) | collective-permute-done | bytes 4128 | tf_op jit(solution)/shard_map/ppermute | solution.py:25
  51.9 0.3 pad_maximum_fusion.3
  52.2 0.2 slice_subtract_fusion
  52.4 0.4 minimum_multiply_fusion
  52.8 0.5 fusion.2
  53.2 0.8 %fusion.5 = f32[4,16,8,128]{3,2,1,0:T(8,128)} fusion(f32[4,16,8,128]{3,2,1,0:T(8,128)S(1)} %broadcast_select_fusion.1, f32[4,16,8,129]{3,2,1,0:T(8,128)S(1)} %fusion.2), kind=kLoop, calls=%fused_computation.21 | loop fusion | flops 131072 | bytes 1048576 | tf_op jit(solution)/shard_map/sub | solution.py:42
  (30 shorter events, 1.1 us)
Async XLA Ops:
  0.0 3.7 %copy-start = (f32[4,16,8,128]{3,2,1,0:T(8,128)S(1)}, f32[4,16,8,128]{3,2,1,0:T(8,128)}, u32[]{:S(2)}) copy-start(f32[4,16,8,128]{3,2,1,0:T(8,128)} %param.3) | copy-start | bytes 786436
  1.2 5.8 %collective-permute-start = (f32[3,16,8,1]{3,2,1,0:T(8,128)S(1)}, f32[3,16,8,1]{3,2,1,0:T(8,128)S(1)}, u32[]{:S(2)}, u32[]{:S(2)}) collective-permute-start(f32[3,16,8,1]{3,2,1,0:T(8,128)S(1)} %get-tuple-element.16), channel_id=1, source_target_pairs={{0,8},{8,16},{16,24},{24,0},{1,9},{9,17},{17,25},{25,1},{2,10},{10... | collective-permute-start | bytes 4616 | tf_op jit(solution)/shard_map/ppermute | solution.py:25
  1.7 7.2 %collective-permute-start.1 = (f32[3,16,8,1]{3,2,1,0:T(8,128)S(1)}, f32[3,16,8,1]{3,2,1,0:T(8,128)S(1)}, u32[]{:S(2)}, u32[]{:S(2)}) collective-permute-start(f32[3,16,8,1]{3,2,1,0:T(8,128)S(1)} %get-tuple-element.17), channel_id=1, source_target_pairs={{8,0},{16,8},{24,16},{0,24},{9,1},{17,9},{25,17},{1,25},{10,2},{18... | collective-permute-start | bytes 4616 | tf_op jit(solution)/shard_map/ppermute | solution.py:26
  9.2 7.3 %collective-permute-start.2 = (f32[3,16,1,130]{3,2,1,0:T(1,128)S(1)}, f32[3,16,1,130]{3,2,1,0:T(1,128)S(1)}, u32[]{:S(2)}, u32[]{:S(2)}) collective-permute-start(f32[3,16,1,130]{3,2,1,0:T(1,128)S(1)} %pad_maximum_fusion.6), channel_id=1, source_target_pairs={{0,1},{1,2},{2,3},{3,4},{4,5},{5,6},{6,7},{7,0},{8,9},{9,10},{10,1... | collective-permute-start | bytes 74888 | tf_op jit(solution)/shard_map/ppermute | solution.py:25
  16.7 4.1 %collective-permute-start.3 = (f32[3,16,1,130]{3,2,1,0:T(1,128)S(1)}, f32[3,16,1,130]{3,2,1,0:T(1,128)S(1)}, u32[]{:S(2)}, u32[]{:S(2)}) collective-permute-start(f32[3,16,1,130]{3,2,1,0:T(1,128)S(1)} %get-tuple-element.8), channel_id=1, source_target_pairs={{1,0},{2,1},{3,2},{4,3},{5,4},{6,5},{7,6},{0,7},{9,8},{10,9},{11,1... | collective-permute-start | bytes 74888 | tf_op jit(solution)/shard_map/ppermute | solution.py:26
  21.8 0.7 %copy-start.2 = (s32[16,8]{0,1:T(8,128)S(1)}, s32[16,8]{0,1:T(8,128)}, u32[]{:S(2)}) copy-start(s32[16,8]{0,1:T(8,128)} %param.4) | copy-start | bytes 1540
  21.8 5.8 %collective-permute-start.4 = (f32[4,16,8,128]{3,2,1,0:T(8,128)S(1)}, f32[4,16,8,128]{3,2,1,0:T(8,128)S(1)}, u32[]{:S(2)}, u32[]{:S(2)}) collective-permute-start(f32[4,16,8,128]{3,2,1,0:T(8,128)S(1)} %pad_maximum_fusion.5), channel_id=1, source_target_pairs={{24,0},{0,8},{8,16},{16,24},{25,1},{1,9},{9,17},{17,25},{26,2},{2,... | collective-permute-start | bytes 786440 | tf_op jit(solution)/shard_map/ppermute | solution.py:15
  30.1 5.8 %collective-permute-start.5 = (f32[4,16,8,128]{3,2,1,0:T(8,128)S(1)}, f32[4,16,8,128]{3,2,1,0:T(8,128)S(1)}, u32[]{:S(2)}, u32[]{:S(2)}) collective-permute-start(f32[4,16,8,128]{3,2,1,0:T(8,128)S(1)} %slice_select_fusion), channel_id=1, source_target_pairs={{24,0},{0,8},{8,16},{16,24},{25,1},{1,9},{9,17},{17,25},{26,2},{2,... | collective-permute-start | bytes 786440 | tf_op jit(solution)/shard_map/ppermute | solution.py:15
  36.0 2.1 %copy-start.1 = (f32[16,8]{0,1:T(8,128)S(1)}, f32[16,8]{0,1:T(8,128)}, u32[]{:S(2)}) copy-start(f32[16,8]{0,1:T(8,128)} %param.5) | copy-start | bytes 1540
  36.0 7.8 %collective-permute-start.6 = (f32[4,16,8,128]{3,2,1,0:T(8,128)S(1)}, f32[4,16,8,128]{3,2,1,0:T(8,128)S(1)}, u32[]{:S(2)}, u32[]{:S(2)}) collective-permute-start(f32[4,16,8,128]{3,2,1,0:T(8,128)S(1)} %broadcast_select_fusion), channel_id=1, source_target_pairs={{16,0},{24,8},{0,16},{8,24},{17,1},{25,9},{1,17},{9,25},{18,2},{26... | collective-permute-start | bytes 786440 | tf_op jit(solution)/shard_map/ppermute | solution.py:15
  44.1 7.8 %collective-permute-start.7 = (f32[4,16,8,2]{3,2,1,0:T(8,128)S(1)}, f32[4,16,8,2]{3,2,1,0:T(8,128)S(1)}, u32[]{:S(2)}, u32[]{:S(2)}) collective-permute-start(f32[4,16,8,2]{3,2,1,0:T(8,128)S(1)} %get-tuple-element.14), channel_id=1, source_target_pairs={{0,8},{8,16},{16,24},{24,0},{1,9},{9,17},{17,25},{25,1},{2,10},{10... | collective-permute-start | bytes 12296 | tf_op jit(solution)/shard_map/ppermute | solution.py:25
  44.1 7.8 %collective-permute-start.8 = (f32[4,16,8,2]{3,2,1,0:T(8,128)S(1)}, f32[4,16,8,2]{3,2,1,0:T(8,128)S(1)}, u32[]{:S(2)}, u32[]{:S(2)}) collective-permute-start(f32[4,16,8,2]{3,2,1,0:T(8,128)S(1)} %get-tuple-element.15), channel_id=1, source_target_pairs={{8,0},{16,8},{24,16},{0,24},{9,1},{17,9},{25,17},{1,25},{10,2},{18... | collective-permute-start | bytes 12296 | tf_op jit(solution)/shard_map/ppermute | solution.py:26
where the time goes:
time: 54.4 us; the launch traced here: 54.1 us
  waiting for transfers between devices  34.8 us (64%)
  starting transfers between devices  9.77 us (18%)
  other arithmetic  5.27 us (10%)
  local copies, waits for them, and re-layouts  3.92 us (7%)
    ppermute x3, waiting for transfers between devices, passed_along(): return lax.ppermute(block, axis, route)  15.8 us
    ppermute x3, waiting for transfers between devices, with_halo(): before = lax.ppermute(last, axis, up)  14.7 us
    ppermute x3, starting transfers between devices, with_halo(): after = lax.ppermute(leading, axis, down)  5.5 us
    ppermute x3, waiting for transfers between devices, with_halo(): after = lax.ppermute(leading, axis, down)  4.26 us
    ppermute x3, starting transfers between devices, with_halo(): before = lax.ppermute(last, axis, up)  2.17 us
    ppermute x3, starting transfers between devices, passed_along(): return lax.ppermute(block, axis, route)  2.09 us
    select_n x7, other arithmetic, barrel_roll(): values = jnp.where(chosen[:, :, None], rolled, values)  1.5 us
    slice x2, local copies, waits for them, and re-layouts, with_halo(): last = lax.slice_in_dim(x, length - width, length, axis=dim)  1.31 us
  transfers between devices with their start and end apart: 9, of which 8 were waited for; matrix products, arithmetic and copies ran while one was open for 2% of the time, Pallas kernels for 0%

commit v1 on v0

v1 whole, which is shorter than its diff:
```python
import functools
import math

import jax
import jax.numpy as jnp
from jax import lax
from jax.experimental import pallas as pl
from jax.experimental.pallas import tpu as pltpu
from jax.sharding import PartitionSpec as P

inner_radius = 0.4
adiabatic = 1.4
MESH = pl.DeviceIdType.MESH
OFFSETS = (-2, -1, 0, 1)
CHUNKS = 4


def remote(src, dst, send, recv, az, rad):
    return pltpu.make_async_remote_copy(
        src_ref=src,
        dst_ref=dst,
        send_sem=send,
        recv_sem=recv,
        device_id={"az": az, "rad": rad},
        device_id_type=MESH,
    )


def minmod(a, b):
    return jnp.maximum(jnp.minimum(a, b), 0.0) + jnp.minimum(jnp.maximum(a, b), 0.0)


def kernel(n, rn, fields, shifts, courant, out, G, H, E, SEG, LANE, CA,
           local_sem, xs, xr, hs, hr, cs, cr, fs, fr):
    _, T, R, L = fields.shape
    X = n // 2
    K = xs.shape[0]
    tc = T // K
    az = lax.axis_index("az")
    rad = lax.axis_index("rad")
    x, c = az // 2, az % 2
    mate = x * 2 + (1 - c)

    def column(k):
        return lax.rem(x + k, X) * 2 + c

    def source(k, core):
        return lax.rem(x + X - k, X) * 2 + core

    has_low, has_high = rad > 0, rad < rn - 1
    sends = (has_high, has_low)
    receives = (has_low, has_high)
    toward = (rad + 1, rad - 1)

    local = pltpu.make_async_copy(fields, G.at[az], local_sem)
    local.start()

    barrier = pltpu.get_barrier_semaphore()

    def greet(a, r):
        pl.semaphore_signal(barrier, inc=1, device_id={"az": a, "rad": r}, device_id_type=MESH)

    greet(mate, rad)
    for k in range(1, X):
        greet(column(k), rad)
    for way in range(2):
        @pl.when(sends[way])
        def _():
            for k in range(X):
                greet(column(k), toward[way])
    neighbours = has_low.astype(jnp.int32) + has_high.astype(jnp.int32)

    local.wait()
    for f in range(3):
        E[0, f] = G[az, f, :, R - 1, :]
        E[1, f] = G[az, f, :, 0, :]

    pl.semaphore_wait(barrier, X + X * neighbours)

    def block(ref, seg, j):
        return ref.at[seg, :, pl.ds(j * tc, tc)]

    def field_copy(j, k):
        return remote(block(G, az, j), block(G, az, j), xs.at[j, k - 1], xr.at[j, k - 1], column(k), rad)

    def field_arrival(j, k):
        seg = source(k, c)
        return remote(block(G, seg, j), block(G, seg, j), xs.at[j, k - 1], xr.at[j, k - 1], column(k), rad)

    def edge_copy(way, k):
        return remote(E.at[way], H.at[way, az], hs.at[way, k], hr.at[way, k], column(k), toward[way])

    def edge_arrival(way, k):
        return remote(E.at[way], H.at[way, source(k, c)], hs.at[way, k], hr.at[way, k], column(k), rad)

    def mate_copy(j, k):
        seg = source(k, c)
        return remote(block(G, seg, j), block(G, seg, j), cs.at[j, k], cr.at[j, k], mate, rad)

    def mate_arrival(j, k):
        seg = source(k, 1 - c)
        return remote(block(G, seg, j), block(G, seg, j), cs.at[j, k], cr.at[j, k], mate, rad)

    def mate_edge(way, k):
        seg = source(k, c)
        return remote(H.at[way, seg], H.at[way, seg], fs.at[way, k], fr.at[way, k], mate, rad)

    def mate_edge_arrival(way, k):
        seg = source(k, 1 - c)
        return remote(H.at[way, seg], H.at[way, seg], fs.at[way, k], fr.at[way, k], mate, rad)

    for way in range(2):
        @pl.when(sends[way])
        def _():
            for k in range(X - 1, -1, -1):
                edge_copy(way, k).start()
    for j in range(K):
        for k in range(1, X):
            field_copy(j, k).start()
    for j in range(K):
        mate_copy(j, 0).start()

    for way in range(2):
        @pl.when(jnp.logical_not(receives[way]))
        def _():
            H[way] = jnp.zeros(H.shape[1:], jnp.float32)

    phi_count, rad_count = n * L, rn * R
    phi_step = 2.0 * math.pi / phi_count
    rad_step = 1.0 / rad_count
    spacing = min(rad_step, inner_radius * phi_step)
    dt = 0.2 * spacing
    viscosity = 0.05 * spacing * spacing / dt
    row = lax.broadcasted_iota(jnp.int32, (R, L), 0)
    lane = lax.broadcasted_iota(jnp.int32, (R, L), 1)
    radius = inner_radius + ((rad * R + row).astype(jnp.float32) + 0.5) * (1.0 / rad_count)
    width = radius * phi_step
    inv_r = 1.0 / radius
    inv_w = 1.0 / width
    spread_az = (dt * viscosity) * inv_w * inv_w
    spread_rad = dt * viscosity / (rad_step * rad_step)
    press_rad = dt * (adiabatic - 1.0) * 0.5 / rad_step
    press_az = (dt * (adiabatic - 1.0) * 0.5) * inv_w
    turn = dt * inv_r
    pull = dt * inv_r * inv_r
    heat = dt * (adiabatic - 1.0)
    heat_rad = heat * 0.5 / rad_step
    heat_az = (heat * 0.5) * inv_w
    heat_r = heat * inv_r
    bits = L.bit_length() - 1

    diagonal = lax.broadcasted_iota(jnp.int32, (R, R), 0) == lax.broadcasted_iota(jnp.int32, (R, R), 1)

    def as_column(values):
        spread = jnp.where(diagonal, jnp.broadcast_to(values, (R, R)), 0.0)
        return jnp.broadcast_to(jnp.sum(spread, axis=1, keepdims=True), (R, L))

    def prepare(t, carry):
        moves = as_column(shifts[pl.ds(t, 1), :].astype(jnp.float32)).astype(jnp.int32)
        cour = as_column(courant[pl.ds(t, 1), :])
        CA[t] = jnp.abs(cour)
        sign = jnp.where(cour >= 0.0, 1, -1)
        for o, offset in enumerate(OFFSETS):
            s = moves - sign * offset
            s = jnp.where(s < 0, s + phi_count, s)
            s = jnp.where(s >= phi_count, s - phi_count, s)
            q = s >> bits
            rest = s & (L - 1)
            seg = az - q - jnp.where(lane + rest >= L, 1, 0)
            SEG[t, o] = jnp.where(seg < 0, seg + n, seg)
            LANE[t, o] = (lane - rest) & (L - 1)
        return carry

    lax.fori_loop(0, T, prepare, 0)

    first_lane, last_lane = lane == 0, lane == L - 1
    low_own = (row == 0) & jnp.logical_not(has_low)
    high_own = (row == R - 1) & jnp.logical_not(has_high)
    low_halo = (row == 0) & has_low
    high_halo = (row == R - 1) & has_high

    def step(t, carry):
        raw = [[G[s, f, t] for f in range(4)] for s in range(n)]
        moved = []
        for s in range(n):
            before, here, after = raw[s - 1], raw[s], raw[(s + 1) % n]
            vr, vp, en, den = here

            def around(f):
                q = here[f]
                left = pltpu.roll(jnp.where(last_lane, before[f], q), 1, 1)
                right = pltpu.roll(jnp.where(first_lane, after[f], q), L - 1, 1)
                low = jnp.where(low_own, q, pltpu.roll(q, 1, 0))
                low = jnp.where(low_halo, H[0, s, f, pl.ds(t, 1), :], low)
                high = jnp.where(high_own, q, pltpu.roll(q, R - 1, 0))
                high = jnp.where(high_halo, H[1, s, f, pl.ds(t, 1), :], high)
                return left, right, low, high

            vl, vh, vd, vu = around(0)
            pl_, ph, pd, pu = around(1)
            el, eh, ed, eu = around(2)
            inv_den = 1.0 / den
            new_r = vr + (
                spread_az * (vh + vl - 2.0 * vr)
                + spread_rad * (vu + vd - 2.0 * vr)
                + (vp * vp * turn - pull)
                - press_rad * (eu - ed) * inv_den
            )
            new_p = vp + (
                spread_az * (ph + pl_ - 2.0 * vp)
                + spread_rad * (pu + pd - 2.0 * vp)
                - vr * vp * turn
                - press_az * (eh - el) * inv_den
            )
            new_e = en - en * (heat_rad * (vu - vd) + heat_az * (ph - pl_) + heat_r * vr)
            moved.append((new_r, new_p, new_e, den))
        amount = CA[t]
        half = 0.5 * (1.0 - amount)
        taken = [[] for _ in range(4)]
        for o in range(len(OFFSETS)):
            seg, at = SEG[t, o], LANE[t, o]
            chosen = [seg == s for s in range(n - 1)]
            for f in range(4):
                value = moved[n - 1][f]
                for s in range(n - 1):
                    value = jnp.where(chosen[s], moved[s][f], value)
                taken[f].append(jnp.take_along_axis(value, at, axis=1, mode="promise_in_bounds"))
        for f in range(4):
            q0, q1, q2, q3 = taken[f]
            d0, d1, d2 = q1 - q0, q2 - q1, q3 - q2
            enters = q1 + half * minmod(d0, d1)
            leaves = q2 + half * minmod(d1, d2)
            out[f, t] = q2 - amount * (leaves - enters)
        return carry

    def finish(j):
        for k in range(X):
            mate_arrival(j, k).wait_recv()
        lax.fori_loop(j * tc, (j + 1) * tc, step, 0)

    for way in range(2):
        @pl.when(receives[way])
        def _():
            for k in range(X):
                edge_arrival(way, k).wait_recv()
                mate_edge(way, k).start()
    for j in range(K):
        for k in range(1, X):
            field_arrival(j, k).wait_recv()
            mate_copy(j, k).start()
        if j == 0:
            for way in range(2):
                @pl.when(receives[way])
                def _():
                    for k in range(X):
                        mate_edge_arrival(way, k).wait_recv()
        else:
            finish(j - 1)
    finish(K - 1)

    for way in range(2):
        @pl.when(sends[way])
        def _():
            for k in range(X):
                edge_copy(way, k).wait_send()

        @pl.when(receives[way])
        def _():
            for k in range(X):
                mate_edge(way, k).wait_send()
    for j in range(K):
        for k in range(1, X):
            field_copy(j, k).wait_send()
        for k in range(X):
            mate_copy(j, k).wait_send()


def shards(fields, shifts, courant):
    n, rn = lax.axis_size("az"), lax.axis_size("rad")
    F, T, R, L = fields.shape
    X = n // 2
    K = math.gcd(T, CHUNKS)
    dma = pltpu.SemaphoreType.DMA
    vmem = pl.BlockSpec(memory_space=pltpu.VMEM)
    return pl.pallas_call(
        functools.partial(kernel, n, rn),
        out_shape=jax.ShapeDtypeStruct(fields.shape, jnp.float32),
        in_specs=[pl.BlockSpec(memory_space=pl.ANY), vmem, vmem],
        out_specs=vmem,
        scratch_shapes=[
            pltpu.VMEM((n, F, T, R, L), jnp.float32),
            pltpu.VMEM((2, n, 3, T, L), jnp.float32),
            pltpu.VMEM((2, 3, T, L), jnp.float32),
            pltpu.VMEM((T, 4, R, L), jnp.int32),
            pltpu.VMEM((T, 4, R, L), jnp.int32),
            pltpu.VMEM((T, R, L), jnp.float32),
            dma(()),
            dma((K, X - 1)), dma((K, X - 1)),
            dma((2, X)), dma((2, X)),
            dma((K, X)), dma((K, X)),
            dma((2, X)), dma((2, X)),
        ],
        compiler_params=pltpu.CompilerParams(collective_id=0, has_side_effects=True),
    )(fields, shifts, courant)


def solution(mesh):
    return jax.shard_map(
        shards,
        mesh=mesh,
        in_specs=(P(None, None, "rad", "az"), P(None, "rad"), P(None, "rad")),
        out_specs=P(None, None, "rad", "az"),
        check_vma=False,
    )
```

time: 54.4 us -> 19.3 us (0.35)
  waiting for transfers between devices: 34.8 us -> 0 us
  Pallas kernels: 0 us -> 15.3 us
  starting transfers between devices: 9.77 us -> 0 us
  other arithmetic: 5.27 us -> 0 us
    ppermute x9 -> x0, waiting for transfers between devices: 34.8 us -> none  [the longest x3 15.8 us: passed_along(): return lax.ppermute(block, axis, route)]
    pallas_call x0 -> x1, Pallas kernels: none -> 15.3 us  [shards(): pl.pallas_call(functools.partial(kernel, n, rn), out_shape=jax.ShapeDtype...]
    ppermute x9 -> x0, starting transfers between devices: 9.77 us -> none  [the longest x3 5.5 us: with_halo(): after = lax.ppermute(leading, axis, down)]
    unnamed x7 -> x5, local copies, waits for them, and re-layouts: 0.67 us -> 3.71 us
    select_n x12 -> x0, other arithmetic: 2.38 us -> none  [the longest x7 1.5 us: barrel_roll(): values = jnp.where(chosen[:, :, None], rolled, values)]
    slice x11 -> x0, local copies, waits for them, and re-layouts: 2.19 us -> none  [the longest x2 1.31 us: with_halo(): last = lax.slice_in_dim(x, length - width, length, axis=dim)]
    sub x2 -> x0, other arithmetic: 1.04 us -> none  [the longest x1 0.84 us: limited(): return extended[..., 2:-2] - (face_flux[..., 1:] - face_flux[..., :-1])]
    concatenate x4 -> x0, other arithmetic: 0.91 us -> none  [the longest x2 0.49 us: with_halo(): x = jnp.concatenate([before, x, after], axis=dim)]
  transfers between devices with their start and end apart: 9 -> 0, of which waited for: 8 -> 0; matrix products, arithmetic and copies ran while one was open for 2% -> 0% of each run, Pallas kernels for 0% -> 0%
where the time goes in v1:
time: 19.3 us; the launch traced here: 19 us
  Pallas kernels  15.3 us (79%)
  local copies, waits for them, and re-layouts  3.71 us (19%)
    pallas_call x1, Pallas kernels, shards(): pl.pallas_call(functools.partial(kernel, n, rn), out_shape=jax.ShapeDtype...  15.3 us
    unnamed x5, local copies, waits for them, and re-layouts  3.71 us

profile of v1, /device:TPU:0, one launch (start us, length us, event | category | flops | bytes accessed | tf_op | source)
XLA Modules:
  0.0 19.0 jit_solution(10053670161707699474)
XLA Ops:
  0.0 0.0 copy-start
  0.0 1.4 %copy.4.shifts = s32[16,8]{1,0:T(8,128)} copy(s32[16,8]{0,1:T(8,128)} %param.4) | data formatting | bytes 1024 | tf_op args[1]
  1.4 0.0 copy-done
  1.4 0.7 %copy.5.courant = f32[16,8]{1,0:T(8,128)} copy(f32[16,8]{0,1:T(8,128)S(1)} %copy-done) | data formatting | bytes 1024 | tf_op args[2]
  2.0 15.3 %shard_map.37 = f32[4,16,8,128]{3,2,1,0:T(8,128)} custom-call(f32[4,16,8,128]{3,2,1,0:T(8,128)} %fields.1, s32[16,8]{1,0:T(8,128)} %copy.4.shifts, f32[16,8]{1,0:T(8,128)} %copy.5.courant), custom_call_target="tpu_custom_call" | custom-call | tf_op jit(solution)/shard_map/pallas_call | solution.py:285
  17.3 1.7 %copy.7 = f32[4,16,8,128]{3,2,1,0:T(8,128)} copy(f32[4,16,8,128]{3,2,1,0:T(8,128)} %shard_map.37) | data formatting | bytes 524288
Async XLA Ops:
  0.0 1.4 %copy-start = (f32[16,8]{0,1:T(8,128)S(1)}, f32[16,8]{0,1:T(8,128)}, u32[]{:S(2)}) copy-start(f32[16,8]{0,1:T(8,128)} %param.5) | copy-start | bytes 1540

commit v2 on v1

--- a/solution.py
+++ b/solution.py
@@ -30,8 +30,8 @@
     return jnp.maximum(jnp.minimum(a, b), 0.0) + jnp.minimum(jnp.maximum(a, b), 0.0)
 
 
-def kernel(n, rn, fields, shifts, courant, out, G, H, E, SEG, LANE, CA,
-           local_sem, xs, xr, hs, hr, cs, cr, fs, fr):
+def kernel(n, rn, fields, shifts_in, courant_in, out, G, H, SEG, LANE, CA, shifts, courant,
+           local_sem, small_sem, xs, xr, hs, hr, cs, cr, fs, fr):
     _, T, R, L = fields.shape
     X = n // 2
     K = xs.shape[0]
@@ -54,6 +54,12 @@
 
     local = pltpu.make_async_copy(fields, G.at[az], local_sem)
     local.start()
+    small = (
+        pltpu.make_async_copy(shifts_in, shifts, small_sem.at[0]),
+        pltpu.make_async_copy(courant_in, courant, small_sem.at[1]),
+    )
+    for copy in small:
+        copy.start()
 
     barrier = pltpu.get_barrier_semaphore()
 
@@ -70,10 +76,6 @@
                 greet(column(k), toward[way])
     neighbours = has_low.astype(jnp.int32) + has_high.astype(jnp.int32)
 
-    local.wait()
-    for f in range(3):
-        E[0, f] = G[az, f, :, R - 1, :]
-        E[1, f] = G[az, f, :, 0, :]
 
     pl.semaphore_wait(barrier, X + X * neighbours)
 
@@ -81,21 +83,22 @@
         return ref.at[seg, :, pl.ds(j * tc, tc)]
 
     def field_copy(j, k):
-        return remote(block(G, az, j), block(G, az, j), xs.at[j, k - 1], xr.at[j, k - 1], column(k), rad)
+        return remote(fields.at[:, pl.ds(j * tc, tc)], block(G, az, j), xs.at[j, k - 1], xr.at[j, k - 1], column(k), rad)
 
     def field_arrival(j, k):
         seg = source(k, c)
         return remote(block(G, seg, j), block(G, seg, j), xs.at[j, k - 1], xr.at[j, k - 1], column(k), rad)
 
     def edge_copy(way, k):
-        return remote(E.at[way], H.at[way, az], hs.at[way, k], hr.at[way, k], column(k), toward[way])
+        return remote(fields.at[0:3, :, (R - 1) * (1 - way), :], H.at[way, az], hs.at[way, k], hr.at[way, k], column(k), toward[way])
 
     def edge_arrival(way, k):
-        return remote(E.at[way], H.at[way, source(k, c)], hs.at[way, k], hr.at[way, k], column(k), rad)
+        return remote(H.at[way, az], H.at[way, source(k, c)], hs.at[way, k], hr.at[way, k], column(k), rad)
 
     def mate_copy(j, k):
         seg = source(k, c)
-        return remote(block(G, seg, j), block(G, seg, j), cs.at[j, k], cr.at[j, k], mate, rad)
+        sent = block(G, seg, j) if k else fields.at[:, pl.ds(j * tc, tc)]
+        return remote(sent, block(G, seg, j), cs.at[j, k], cr.at[j, k], mate, rad)
 
     def mate_arrival(j, k):
         seg = source(k, 1 - c)
@@ -149,15 +152,12 @@
     heat_r = heat * inv_r
     bits = L.bit_length() - 1
 
-    diagonal = lax.broadcasted_iota(jnp.int32, (R, R), 0) == lax.broadcasted_iota(jnp.int32, (R, R), 1)
-
-    def as_column(values):
-        spread = jnp.where(diagonal, jnp.broadcast_to(values, (R, R)), 0.0)
-        return jnp.broadcast_to(jnp.sum(spread, axis=1, keepdims=True), (R, L))
-
-    def prepare(t, carry):
-        moves = as_column(shifts[pl.ds(t, 1), :].astype(jnp.float32)).astype(jnp.int32)
-        cour = as_column(courant[pl.ds(t, 1), :])
+    local.wait()
+    for copy in small:
+        copy.wait()
+    for t in range(T):
+        moves = jnp.broadcast_to(shifts[:, t : t + 1], (R, L))
+        cour = jnp.broadcast_to(courant[:, t : t + 1], (R, L))
         CA[t] = jnp.abs(cour)
         sign = jnp.where(cour >= 0.0, 1, -1)
         for o, offset in enumerate(OFFSETS):
@@ -169,9 +169,6 @@
             seg = az - q - jnp.where(lane + rest >= L, 1, 0)
             SEG[t, o] = jnp.where(seg < 0, seg + n, seg)
             LANE[t, o] = (lane - rest) & (L - 1)
-        return carry
-
-    lax.fori_loop(0, T, prepare, 0)
 
     first_lane, last_lane = lane == 0, lane == L - 1
     low_own = (row == 0) & jnp.logical_not(has_low)
@@ -280,28 +277,31 @@
     F, T, R, L = fields.shape
     X = n // 2
     K = math.gcd(T, CHUNKS)
+    held = (n + 2) * F * T * R * L + 2 * n * 3 * T * L + 9 * T * R * L
+    grant = 4 * held + (2 << 20)
     dma = pltpu.SemaphoreType.DMA
     vmem = pl.BlockSpec(memory_space=pltpu.VMEM)
     return pl.pallas_call(
         functools.partial(kernel, n, rn),
         out_shape=jax.ShapeDtypeStruct(fields.shape, jnp.float32),
-        in_specs=[pl.BlockSpec(memory_space=pl.ANY), vmem, vmem],
+        in_specs=[pl.BlockSpec(memory_space=pltpu.HBM)] * 3,
         out_specs=vmem,
         scratch_shapes=[
             pltpu.VMEM((n, F, T, R, L), jnp.float32),
             pltpu.VMEM((2, n, 3, T, L), jnp.float32),
-            pltpu.VMEM((2, 3, T, L), jnp.float32),
             pltpu.VMEM((T, 4, R, L), jnp.int32),
             pltpu.VMEM((T, 4, R, L), jnp.int32),
             pltpu.VMEM((T, R, L), jnp.float32),
-            dma(()),
+            pltpu.VMEM((R, T), jnp.int32),
+            pltpu.VMEM((R, T), jnp.float32),
+            dma(()), dma((2,)),
             dma((K, X - 1)), dma((K, X - 1)),
             dma((2, X)), dma((2, X)),
             dma((K, X)), dma((K, X)),
             dma((2, X)), dma((2, X)),
         ],
-        compiler_params=pltpu.CompilerParams(collective_id=0, has_side_effects=True),
-    )(fields, shifts, courant)
+        compiler_params=pltpu.CompilerParams(collective_id=0, has_side_effects=True, vmem_limit_bytes=grant),
+    )(*(pltpu.with_memory_space_constraint(v, pltpu.HBM) for v in (fields, shifts.T, courant.T)))
 
 
 def solution(mesh):

time: 19.3 us -> 15 us (0.78)
  local copies, waits for them, and re-layouts: 3.71 us -> 0.71 us
  Pallas kernels: 15.3 us -> 14.1 us
    unnamed x5 -> x1, local copies, waits for them, and re-layouts: 3.71 us -> 0.71 us
    pallas_call x1, Pallas kernels: 15.3 us -> 14.1 us  [shards(): pl.pallas_call(functools.partial(kernel, n, rn), out_shape=jax.ShapeDtype...]
where the time goes in v2:
time: 15 us; the launch traced here: 14.8 us
  Pallas kernels  14.1 us (94%)
  local copies, waits for them, and re-layouts  0.71 us (5%)
    pallas_call x1, Pallas kernels, shards(): pl.pallas_call(functools.partial(kernel, n, rn), out_shape=jax.ShapeDtype...  14.1 us
    unnamed x1, local copies, waits for them, and re-layouts  0.71 us

profile of v2, /device:TPU:0, one launch (start us, length us, event | category | flops | bytes accessed | tf_op | source)
XLA Modules:
  0.0 14.8 jit_solution(3718984987653867545)
XLA Ops:
  0.0 14.1 %shard_map.37 = f32[4,16,8,128]{3,2,1,0:T(8,128)S(1)} custom-call(f32[4,16,8,128]{3,2,1,0:T(8,128)} %fields.1, s32[8,16]{1,0:T(8,128)} %bitcast.2, f32[8,16]{1,0:T(8,128)} %bitcast.3), custom_call_target="tpu_custom_call" | custom-call | tf_op jit(solution)/shard_map/pallas_call | solution.py:284
  14.1 0.7 %copy.5 = f32[4,16,8,128]{3,2,1,0:T(8,128)} copy(f32[4,16,8,128]{3,2,1,0:T(8,128)S(1)} %shard_map.37) | data formatting | bytes 524288

commit v3 on v2

--- a/solution.py
+++ b/solution.py
@@ -233,7 +233,12 @@
     def finish(j):
         for k in range(X):
             mate_arrival(j, k).wait_recv()
-        lax.fori_loop(j * tc, (j + 1) * tc, step, 0)
+        def group(i, carry):
+            for u in range(2):
+                carry = step(2 * i + u, carry)
+            return carry
+
+        lax.fori_loop(j * (tc // 2), (j + 1) * (tc // 2), group, 0)
 
     for way in range(2):
         @pl.when(receives[way])
@@ -241,19 +246,27 @@
             for k in range(X):
                 edge_arrival(way, k).wait_recv()
                 mate_edge(way, k).start()
-    for j in range(K):
-        for k in range(1, X):
-            field_arrival(j, k).wait_recv()
-            mate_copy(j, k).start()
-        if j == 0:
-            for way in range(2):
-                @pl.when(receives[way])
-                def _():
-                    for k in range(X):
-                        mate_edge_arrival(way, k).wait_recv()
-        else:
+
+    def turn_over(j, carry):
+        @pl.when(j < K)
+        def _():
+            for k in range(1, X):
+                field_arrival(j, k).wait_recv()
+                mate_copy(j, k).start()
+
+        for way in range(2):
+            @pl.when((j == 1) & receives[way])
+            def _():
+                for k in range(X):
+                    mate_edge_arrival(way, k).wait_recv()
+
+        @pl.when(j > 0)
+        def _():
             finish(j - 1)
-    finish(K - 1)
+
+        return carry
+
+    lax.fori_loop(0, K + 1, turn_over, 0)
 
     for way in range(2):
         @pl.when(sends[way])

time: 15 us -> 14.4 us (0.960)
  Pallas kernels: 14.1 us -> 13.5 us
    pallas_call x1, Pallas kernels: 14.1 us -> 13.5 us  [shards(): pl.pallas_call(functools.partial(kernel, n, rn), out_shape=jax.ShapeDtype...]
where the time goes in v3:
time: 14.4 us; the launch traced here: 14.2 us
  Pallas kernels  13.5 us (94%)
  local copies, waits for them, and re-layouts  0.71 us (5%)
    pallas_call x1, Pallas kernels, shards(): pl.pallas_call(functools.partial(kernel, n, rn), out_shape=jax.ShapeDtype...  13.5 us
    unnamed x1, local copies, waits for them, and re-layouts  0.71 us

profile of v3, /device:TPU:0, one launch (start us, length us, event | category | flops | bytes accessed | tf_op | source)
XLA Modules:
  0.0 14.2 jit_solution(3156237168431457172)
XLA Ops:
  0.0 13.5 %shard_map.37 = f32[4,16,8,128]{3,2,1,0:T(8,128)S(1)} custom-call(f32[4,16,8,128]{3,2,1,0:T(8,128)} %fields.1, s32[8,16]{1,0:T(8,128)} %bitcast.2, f32[8,16]{1,0:T(8,128)} %bitcast.3), custom_call_target="tpu_custom_call" | custom-call | tf_op jit(solution)/shard_map/pallas_call | solution.py:297
  13.5 0.7 %copy.5 = f32[4,16,8,128]{3,2,1,0:T(8,128)} copy(f32[4,16,8,128]{3,2,1,0:T(8,128)S(1)} %shard_map.37) | data formatting | bytes 524288
